TPU v7x, 32 devices: a whole 2x2x4 slice. The times are simulated.
32 devices in a mesh: frame: 16 (over z, y, x), head: 2 (over core).
Axes of the slice: x: 2, y: 2, z: 4, core: 2. Of those that a mesh axis runs over, the one named last changes fastest.
Arguments:
- residual: bfloat16 [2048, 5120], P('frame', 'head'), may hold values from -48 to 48
- query_proj: bfloat16 [2048, 3072], P('frame', 'head'), may hold values from -200 to 200
- key_proj: bfloat16 [2048, 3072], P('frame', 'head'), may hold values from -200 to 200
- value_proj: bfloat16 [2048, 3072], P('frame', 'head'), may hold values from -6 to 6
- q_gain: float32 [3072], P('head'), may hold values from 1 to 3
- k_gain: float32 [3072], P('head'), may hold values from 1 to 3
- time_embed: float32 [5120], P(('frame', 'head')), may hold values from -6 to 6
- time_proj: bfloat16 [5120, 3, 5120], P(('frame', 'head')), may hold values from -0.15625 to 0.15625
- mod_table: float32 [3, 5120], P(None, 'head'), may hold values from -3 to 3
- out_weight: bfloat16 [3072, 5120], P('head'), may hold values from -0.109375 to 0.109375
Outputs:
- hidden_out: bfloat16 [2048, 5120], P('frame', 'head')
- mlp_input: bfloat16 [2048, 5120], P('frame', 'head')
All inputs are finite; a program needn't handle non-finite values.
Results may differ from a plain program's by a relative error of at most 0.0071.
Values may be sent and summed in bfloat16 or wider, within the bound.
A program may use at most 128 MiB of HBM per device.

v0:
```python
import math
import jax
import jax.numpy as jnp
from jax import lax
from jax.sharding import PartitionSpec as P

D = 5120
HEADS = 24
HD = 128


def accumulate(carry, queries, keys_block, values_block):
    count = keys_block.shape[0]
    heads_here = queries.shape[1]
    keys_three = keys_block.reshape(count, heads_here, HD)
    values_three = values_block.reshape(count, heads_here, HD).astype(jnp.float32)
    scores = jnp.einsum("thd,shd->ths", queries, keys_three, preferred_element_type=jnp.float32) * (
        1.0 / math.sqrt(HD)
    )
    top_old, total_old, summed = carry
    top_new = jnp.maximum(top_old, jnp.max(scores, axis=2))
    weights = jnp.exp(scores - top_new[:, :, None])
    total_new = jnp.sum(weights, axis=2)
    summed_new = jnp.einsum("ths,shd->thd", weights, values_three, precision=lax.Precision.HIGHEST)
    return (top_new, total_new, summed_new)


def shards(
    residual,
    query_proj,
    key_proj,
    value_proj,
    q_gain,
    k_gain,
    time_embed,
    time_proj,
    mod_table,
    out_weight,
):
    emb = jax.nn.silu(time_embed)
    partial_mod = jnp.einsum(
        "r,rcd->cd", emb, time_proj.astype(jnp.float32), precision=lax.Precision.HIGHEST
    )
    width = mod_table.shape[1]
    summed_mod = lax.psum(partial_mod, ("frame", "head"))
    share = lax.dynamic_slice_in_dim(summed_mod, lax.axis_index("head") * width, width, 1)
    modulation = mod_table + share
    gate = modulation[0]
    shift = modulation[1]
    scale = modulation[2]
    tok_rows = query_proj.shape[0]
    heads_here = query_proj.shape[1] // HD
    query_wide = query_proj.astype(jnp.float32)
    key_wide = key_proj.astype(jnp.float32)
    total_q, total_k = lax.psum(
        (jnp.sum(query_wide * query_wide, axis=1), jnp.sum(key_wide * key_wide, axis=1)), "head"
    )
    query_rms = lax.rsqrt(total_q / (HEADS * HD) + 1e-06)
    key_rms = lax.rsqrt(total_k / (HEADS * HD) + 1e-06)
    queries = (
        (query_wide * query_rms[:, None] * q_gain)
        .astype(jnp.bfloat16)
        .reshape(tok_rows, heads_here, HD)
    )
    start_state = (
        jnp.full((tok_rows, heads_here), -1e30, jnp.float32),
        jnp.zeros((tok_rows, heads_here), jnp.float32),
        jnp.zeros((tok_rows, heads_here, HD), jnp.float32),
    )
    every_scale = lax.all_gather(key_rms, "frame", axis=0, tiled=True)
    keys_block = (
        lax.all_gather(key_proj, "frame", axis=0, tiled=True).astype(jnp.float32)
        * every_scale[:, None]
        * k_gain
    ).astype(jnp.bfloat16)
    top_final, total_final, summed_final = accumulate(
        start_state, queries, keys_block, lax.all_gather(value_proj, "frame", axis=0, tiled=True)
    )
    attn = (
        (summed_final / total_final[:, :, None])
        .astype(jnp.bfloat16)
        .reshape(tok_rows, heads_here * HD)
    )
    proj = (
        lax.psum_scatter(
            lax.dot_general(
                out_weight, attn, (((0,), (1,)), ((), ())), preferred_element_type=jnp.float32
            ).astype(jnp.bfloat16),
            "head",
            scatter_dimension=0,
            tiled=True,
        )
        .astype(jnp.float32)
        .T
    )
    hidden_out = (residual.astype(jnp.float32) + gate * proj).astype(jnp.bfloat16)
    hidden32 = lax.optimization_barrier(hidden_out).astype(jnp.float32)
    row_sum, row_squares = lax.psum(
        (jnp.sum(hidden32, axis=1), jnp.sum(hidden32 * hidden32, axis=1)), "head"
    )
    mean = row_sum[:, None] / D
    var = row_squares[:, None] / D - mean * mean
    mlp_input = ((hidden32 - mean) * lax.rsqrt(var + 1e-06) * (1.0 + scale) + shift).astype(
        jnp.bfloat16
    )
    return (hidden_out, mlp_input)


def solution(mesh):
    in_specs = (
        P("frame", "head"),
        P("frame", "head"),
        P("frame", "head"),
        P("frame", "head"),
        P("head"),
        P("head"),
        P(("frame", "head")),
        P(("frame", "head"), None, None),
        P(None, "head"),
        P("head", None),
    )
    out_specs = (P("frame", "head"), P("frame", "head"))
    return jax.shard_map(shards, mesh=mesh, in_specs=in_specs, out_specs=out_specs, check_vma=False)
```

profile of v0, /device:TPU:0, one launch (start us, length us, event | category | flops | bytes accessed | tf_op | source)
XLA Modules:
  0.0 312.0 jit_solution(16471371955343777573)
XLA Ops:
  7.2 0.0 all-gather.4.cloned.1.call-start
  7.2 1.9 copy.22
  9.1 0.0 all-gather.4.cloned.1.call-update
  9.1 0.0 all-gather.6.cloned.1.call-start
  9.2 0.7 all-gather.6.cloned.1.call-update
  9.9 0.0 reduce-scatter.2.cloned.1.call-start
  9.9 1.2 copy.23
  11.2 1.2 multiply_reduce_fusion
  12.3 0.2 fusion.22
  12.6 2.6 all-reduce.1
  15.2 42.8 %all-gather = f32[16,1,128]{2,1,0:T(1,128)S(1)} all-gather(f32[1,1,128]{2,1,0:T(1,128)S(1)} %rsqrt_bitcast_fusion), channel_id=1, replica_groups=mesh['frame'=16,'head'=2] {'frame'}, dimensions={0}, use_global_device_ids=true | all-gather | bytes 8704 | tf_op jit(solution)/shard_map/all_gather | solution.py:70
  58.0 1.0 fusion.24
  59.0 70.0 %all-gather.4.cloned.1.call-done = bf16[2048,1536]{0,1:T(8,128)(2,1)} async-done(((bf16[128,1536]{0,1:T(8,128)(2,1)}), bf16[2048,1536]{0,1:T(8,128)(2,1)}) %all-gather.4.cloned.1.call-update) | async-done | bytes 6291472 | tf_op jit(solution)/shard_map/all_gather | solution.py:72
  129.0 6.9 %multiply_convert_fusion = bf16[2048,1536]{0,1:T(8,128)(2,1)} fusion(bf16[2048,1536]{0,1:T(8,128)(2,1)} %all-gather.4.cloned.1.call-done, f32[1536]{0:T(1024)} %param.15, f32[2048]{0:T(1024)S(1)} %bitcast.49), kind=kLoop, calls=%fused_computation.3 | loop fusion | flops 12582912 | bytes 12597248 | tf_op jit(solution)/shard_map/convert_element_type | solution.py:75
  135.9 4.7 %bitcast_reduce_fusion = (f32[128,12]{0,1:T(8,128)S(1)}, f32[12,2048,128]{2,1,0:T(8,128)S(1)}) fusion(bf16[2048,12,128]{0,2,1:T(8,128)(2,1)} %bitcast.44, bf16[128,12,128]{0,2,1:T(8,128)(2,1)S(1)} %bitcast.46), kind=kOutput, calls=%fused_computation.1 | convolution fusion | flops 811596288 | bytes 19273728 | tf_op jit(solution)/shard_map/thd,shd->ths/dot_general | solution.py:17
  140.6 0.0 copy-start
  140.6 4.5 %copy-done = f32[12,2048,128]{2,1,0:T(8,128)} copy-done((f32[12,2048,128]{2,1,0:T(8,128)}, f32[12,2048,128]{2,1,0:T(8,128)S(1)}, u32[]{:S(2)}) %copy-start) | copy-done | bytes 12582936
  145.2 2.1 fusion.1
  147.3 76.2 %all-gather.6.cloned.1.call-done = bf16[2048,1536]{1,0:T(8,128)(2,1)} async-done(((bf16[128,1536]{1,0:T(8,128)(2,1)}), bf16[2048,1536]{1,0:T(8,128)(2,1)}) %all-gather.6.cloned.1.call-update) | async-done | bytes 6291472 | tf_op jit(solution)/shard_map/all_gather | solution.py:77
  223.4 8.7 %copy.26 = bf16[2048,1536]{0,1:T(8,128)(2,1)} copy(bf16[2048,1536]{1,0:T(8,128)(2,1)} %all-gather.6.cloned.1.call-done) | data formatting | bytes 12582912 | tf_op jit(solution)/shard_map/all_gather | solution.py:77
  232.1 14.6 %fusion.19 = bf16[128,12,128]{0,2,1:T(8,128)(2,1)S(1)} fusion(bf16[2048,12,128]{0,2,1:T(8,128)(2,1)} %bitcast.45, f32[12,2048,128]{2,1,0:T(8,128)} %copy-done, f32[128,12]{0,1:T(8,128)S(1)} %broadcast_maximum_fusion, f32[128,12]{0,1:T(8,128)S(1)} %fusion.1), kind=kOutput, calls=%fused_computation.24 | convolution fusion | flops 4838522880 | bytes 19279872 | tf_op jit(solution)/shard_map/ths,shd->thd/dot_general | solution.py:24
  246.8 0.0 copy-start.4
  246.8 8.8 %fusion.6 = bf16[5120,128]{0,1:T(8,128)(2,1)} fusion(bf16[128,1536]{0,1:T(8,128)(2,1)S(1)} %bitcast.47, bf16[1536,5120]{1,0:T(8,128)(2,1)} %param.19), kind=kOutput, calls=%fused_computation.9 | convolution fusion | flops 2013921280 | bytes 17432576 | tf_op jit(solution)/shard_map/dot_general | solution.py:86
  255.6 0.0 copy-start.3
  255.6 0.0 copy-start.2
  255.6 0.0 reduce-scatter.2.cloned.1.call-update
  255.6 0.0 copy-done.4
  255.7 4.7 %fusion.27 = f32[1,3,5120]{2,0,1:T(1,128)S(1)} fusion(f32[160,1,1]{0,1,2:T(1,128)S(1)} %bitcast.50, bf16[160,3,5120]{2,0,1:T(8,128)(2,1)} %param.17), kind=kOutput, calls=%fused_computation.42 | convolution fusion | flops 29491200 | bytes 4977280 | tf_op jit(solution)/shard_map/r,rcd->cd/dot_general | solution.py:41
  260.4 39.6 %psum.35 = f32[3,5120]{1,0:T(4,128)S(1)} all-reduce(f32[3,5120]{1,0:T(4,128)S(1)} %bitcast.48), channel_id=1, replica_groups=mesh['frame'=16,'head'=2] {'frame','head'}, use_global_device_ids=true, to_apply=%region_0.1 | all-reduce | flops 15360 | bytes 122880 | tf_op jit(solution)/shard_map/psum | solution.py:45
  300.0 0.0 copy-done.3
  300.0 0.1 fusion.25
  300.1 0.0 reduce-scatter.2.cloned.1.call-done
  300.1 0.0 copy-done.2
  300.1 1.3 fusion.12
  301.4 0.0 copy-start.1
  301.4 0.3 convert_reduce_fusion
  301.7 2.5 all-reduce
  304.2 1.3 fusion.10
  305.5 0.0 copy-done.1
  (7 shorter events, 0.1 us)
Async XLA Ops:
  7.2 121.9 %all-gather.4.cloned.1.call-start = ((), (), s32[]{:S(2)}) async-start(), calls=%async_computation.1 | async-start | bytes 6684672 | tf_op jit(solution)/shard_map/all_gather | solution.py:72
  9.1 214.3 %all-gather.6.cloned.1.call-start = ((), (), s32[]{:S(2)}) async-start(), calls=%async_computation.2 | async-start | bytes 6684672 | tf_op jit(solution)/shard_map/all_gather | solution.py:77
  9.9 290.2 %reduce-scatter.2.cloned.1.call-start = ((), (), s32[]{:S(2)}) async-start(), calls=%async_computation.3 | async-start | bytes 1966080 | tf_op jit(solution)/shard_map/reduce_scatter | solution.py:85
  140.6 4.6 %copy-start = (f32[12,2048,128]{2,1,0:T(8,128)}, f32[12,2048,128]{2,1,0:T(8,128)S(1)}, u32[]{:S(2)}) copy-start(f32[12,2048,128]{2,1,0:T(8,128)S(1)} %get-tuple-element.14) | copy-start | bytes 37748740
  246.8 8.9 %copy-start.4 = (f32[160]{0:T(256)S(1)}, f32[160]{0:T(256)}, u32[]{:S(2)}) copy-start(f32[160]{0:T(256)} %param.16) | copy-start | bytes 1924
  255.6 44.4 %copy-start.3 = (f32[3,2560]{1,0:T(4,128)S(1)}, f32[3,2560]{1,0:T(4,128)}, u32[]{:S(2)}) copy-start(f32[3,2560]{1,0:T(4,128)} %param.18) | copy-start | bytes 92164
  255.6 44.5 %copy-start.2 = (bf16[128,2560]{1,0:T(8,128)(2,1)S(1)}, bf16[128,2560]{1,0:T(8,128)(2,1)}, u32[]{:S(2)}) copy-start(bf16[128,2560]{1,0:T(8,128)(2,1)} %param.10) | copy-start | bytes 1966084
  301.4 4.1 %copy-start.1 = (bf16[128,2560]{1,0:T(8,128)(2,1)}, bf16[128,2560]{1,0:T(8,128)(2,1)S(1)}, u32[]{:S(2)}) copy-start(bf16[128,2560]{1,0:T(8,128)(2,1)S(1)} %fusion.12) | copy-start | bytes 1966084
Sparse Core Ops, SparseCore 0:
  11.2 117.7 all-gather.3
  131.8 91.5 all-gather.5
  255.7 7.1 reduce-scatter.1
where the time goes:
time: 313 us; the launch traced here: 312 us
  waiting for transfers between devices  147 us (47%)
  blocking collectives  87.5 us (28%)
  matrix products  32.8 us (10%)
  local copies, waits for them, and re-layouts  16.4 us (5%)
  other arithmetic  14.3 us (5%)
  between operations  13.9 us (4%)
    all_gather x1, waiting for transfers between devices, shards(): lax.all_gather(value_proj, 'frame', axis=0, tiled=True)  76.2 us
    all_gather x1, waiting for transfers between devices, shards(): lax.all_gather(key_proj, 'frame', axis=0, tiled=True).astype(jnp.float32)  70 us
    all_gather x1, blocking collectives, shards(): every_scale = lax.all_gather(key_rms, 'frame', axis=0, tiled=True)  42.8 us
    psum x1, blocking collectives, shards(): summed_mod = lax.psum(partial_mod, ('frame', 'head'))  39.6 us
    dot_general x1, matrix products, accumulate(): jnp.einsum('ths,shd->thd', weights, values_three, precision=lax.Precision...  14.6 us
    dot_general x1, matrix products, shards(): lax.dot_general(out_weight, attn, (((0,), (1,)), ((), ())), preferred_ele...  8.81 us
    all_gather x1, local copies, waits for them, and re-layouts, shards(): lax.all_gather(value_proj, 'frame', axis=0, tiled=True)  8.7 us
    unnamed x12, local copies, waits for them, and re-layouts  7.7 us
  transfers between devices with their start and end apart: 3, of which 2 were waited for; matrix products, arithmetic and copies ran while one was open for 7% of the time, Pallas kernels for 0%

commit v1 on v0

--- a/solution.py
+++ b/solution.py
@@ -42,7 +42,8 @@
         "r,rcd->cd", emb, time_proj.astype(jnp.float32), precision=lax.Precision.HIGHEST
     )
     width = mod_table.shape[1]
-    summed_mod = lax.psum(partial_mod, ("frame", "head"))
+    parts = lax.all_gather(partial_mod, ("frame", "head"))
+    summed_mod = jnp.sum(parts, axis=0)
     share = lax.dynamic_slice_in_dim(summed_mod, lax.axis_index("head") * width, width, 1)
     modulation = mod_table + share
     gate = modulation[0]

time: 313 us -> 305 us (0.974)
  blocking collectives: 87.5 us -> 48 us
  waiting for transfers between devices: 147 us -> 180 us
    psum x1 -> x0, blocking collectives: 39.6 us -> none  [shards(): summed_mod = lax.psum(partial_mod, ('frame', 'head'))]
    all_gather x0 -> x1, waiting for transfers between devices: none -> 17.7 us  [shards(): parts = lax.all_gather(partial_mod, ('frame', 'head'))]
    all_gather x1, waiting for transfers between devices: 76.2 us -> 87.5 us  [shards(): lax.all_gather(value_proj, 'frame', axis=0, tiled=True)]
    reduce_scatter x1, waiting for transfers between devices: 0.02 us -> 7.32 us  [shards(): lax.psum_scatter(lax.dot_general(out_weight, attn, (((0,), (1,)), ((), ()...]
    all_gather x1, waiting for transfers between devices: 70 us -> 66.8 us  [shards(): lax.all_gather(key_proj, 'frame', axis=0, tiled=True).astype(jnp.float32)]
    unnamed x12 -> x18, local copies, waits for them, and re-layouts: 7.7 us -> 4.71 us
  transfers between devices with their start and end apart: 3 -> 4, of which waited for: 2 -> 4; matrix products, arithmetic and copies ran while one was open for 7% -> 18% of each run, Pallas kernels for 0% -> 0%
where the time goes in v1:
time: 305 us
  waiting for transfers between devices  180 us (59%)
  blocking collectives  48 us (16%)
  matrix products  33.1 us (11%)
  other arithmetic  15.4 us (5%)
  local copies, waits for them, and re-layouts  14 us (5%)
  between operations  13.9 us (5%)
    all_gather x1, waiting for transfers between devices, shards(): lax.all_gather(value_proj, 'frame', axis=0, tiled=True)  87.5 us
    all_gather x1, waiting for transfers between devices, shards(): lax.all_gather(key_proj, 'frame', axis=0, tiled=True).astype(jnp.float32)  66.8 us
    all_gather x1, blocking collectives, shards(): every_scale = lax.all_gather(key_rms, 'frame', axis=0, tiled=True)  42.9 us
    all_gather x1, waiting for transfers between devices, shards(): parts = lax.all_gather(partial_mod, ('frame', 'head'))  17.7 us
    dot_general x1, matrix products, accumulate(): jnp.einsum('ths,shd->thd', weights, values_three, precision=lax.Precision...  14.7 us
    dot_general x1, matrix products, shards(): lax.dot_general(out_weight, attn, (((0,), (1,)), ((), ())), preferred_ele...  9.14 us
    all_gather x1, local copies, waits for them, and re-layouts, shards(): lax.all_gather(value_proj, 'frame', axis=0, tiled=True)  8.62 us
    reduce_scatter x1, waiting for transfers between devices, shards(): lax.psum_scatter(lax.dot_general(out_weight, attn, (((0,), (1,)), ((), ()...  7.32 us
  transfers between devices with their start and end apart: 4, of which 4 were waited for; matrix products, arithmetic and copies ran while one was open for 18% of the time, Pallas kernels for 0%

profile of v1, /device:TPU:0, one launch (start us, length us, event | category | flops | bytes accessed | tf_op | source)
XLA Modules:
  0.0 304.6 jit_solution(2561973870683443484)
XLA Ops:
  7.2 0.0 copy-start.2
  7.2 0.0 copy-start.4
  7.2 0.0 copy-start.6
  7.2 0.0 copy-start.7
  7.2 0.0 all-gather.7.cloned.1.call-start
  7.3 2.0 copy.22
  9.2 0.0 all-gather.7.cloned.1.call-update
  9.2 0.0 all-gather.9.cloned.1.call-start
  9.3 0.7 all-gather.9.cloned.1.call-update
  10.0 0.0 all-gather.11.cloned.1.call-start
  10.0 0.7 divide_multiply_fusion
  10.7 4.4 %fusion.27 = f32[1,3,5120]{2,0,1:T(1,128)S(1)} fusion(f32[160,1,1]{0,1,2:T(1,128)S(1)} %bitcast.47, bf16[160,3,5120]{2,0,1:T(8,128)(2,1)} %param.17), kind=kOutput, calls=%fused_computation.41 | convolution fusion | flops 29491200 | bytes 4977280 | tf_op jit(solution)/shard_map/r,rcd->cd/dot_general | solution.py:41
  15.1 0.7 copy.28
  15.8 0.0 all-gather.11.cloned.1.call-update
  15.8 0.0 reduce-scatter.2.cloned.1.call-start
  15.9 0.0 copy-done.2
  15.9 0.2 multiply_reduce_fusion
  16.1 0.0 copy-done.4
  16.1 0.2 copy.23
  16.3 0.2 fusion.22
  16.5 2.6 all-reduce.1
  19.1 42.9 %all-gather.2 = f32[16,1,128]{2,1,0:T(1,128)S(1)} all-gather(f32[1,1,128]{2,1,0:T(1,128)S(1)} %rsqrt_bitcast_fusion), channel_id=1, replica_groups=mesh['frame'=16,'head'=2] {'frame'}, dimensions={0}, use_global_device_ids=true | all-gather | bytes 8704 | tf_op jit(solution)/shard_map/all_gather | solution.py:71
  62.0 0.0 copy-done.6
  62.0 0.3 fusion.24
  62.3 66.8 %all-gather.7.cloned.1.call-done = bf16[2048,1536]{0,1:T(8,128)(2,1)} async-done(((bf16[128,1536]{0,1:T(8,128)(2,1)}), bf16[2048,1536]{0,1:T(8,128)(2,1)}) %all-gather.7.cloned.1.call-update) | async-done | bytes 6291472 | tf_op jit(solution)/shard_map/all_gather | solution.py:73
  129.1 0.0 copy-done.7
  129.1 6.8 %multiply_convert_fusion = bf16[2048,1536]{0,1:T(8,128)(2,1)} fusion(bf16[2048,1536]{0,1:T(8,128)(2,1)} %all-gather.7.cloned.1.call-done, f32[1536]{0:T(1024)S(1)} %copy-done.7, f32[2048]{0:T(1024)S(1)} %bitcast.46), kind=kLoop, calls=%fused_computation.3 | loop fusion | flops 12582912 | bytes 12597248 | tf_op jit(solution)/shard_map/convert_element_type | solution.py:76
  135.9 87.5 %all-gather.9.cloned.1.call-done = bf16[2048,1536]{1,0:T(8,128)(2,1)} async-done(((bf16[128,1536]{1,0:T(8,128)(2,1)}), bf16[2048,1536]{1,0:T(8,128)(2,1)}) %all-gather.9.cloned.1.call-update) | async-done | bytes 6291472 | tf_op jit(solution)/shard_map/all_gather | solution.py:78
  223.5 8.6 %copy.26 = bf16[2048,1536]{0,1:T(8,128)(2,1)} copy(bf16[2048,1536]{1,0:T(8,128)(2,1)} %all-gather.9.cloned.1.call-done) | data formatting | bytes 12582912 | tf_op jit(solution)/shard_map/all_gather | solution.py:78
  232.1 4.9 %bitcast_reduce_fusion = (f32[128,12]{0,1:T(8,128)S(1)}, f32[12,2048,128]{2,1,0:T(8,128)S(1)}) fusion(bf16[2048,12,128]{0,2,1:T(8,128)(2,1)} %bitcast.42, bf16[128,12,128]{0,2,1:T(8,128)(2,1)S(1)} %bitcast.44), kind=kOutput, calls=%fused_computation.1 | convolution fusion | flops 811596288 | bytes 19273728 | tf_op jit(solution)/shard_map/thd,shd->ths/dot_general | solution.py:17
  237.0 0.0 copy-start
  237.0 2.1 fusion.1
  239.1 2.5 copy-done
  241.6 14.7 %fusion.19 = bf16[128,12,128]{0,2,1:T(8,128)(2,1)S(1)} fusion(bf16[2048,12,128]{0,2,1:T(8,128)(2,1)} %bitcast.43, f32[12,2048,128]{2,1,0:T(8,128)} %copy-done, f32[128,12]{0,1:T(8,128)S(1)} %broadcast_maximum_fusion, f32[128,12]{0,1:T(8,128)S(1)} %fusion.1), kind=kOutput, calls=%fused_computation.24 | convolution fusion | flops 4838522880 | bytes 19279872 | tf_op jit(solution)/shard_map/ths,shd->thd/dot_general | solution.py:24
  256.2 0.0 copy-start.5
  256.2 0.0 copy-start.3
  256.2 9.1 %fusion.6 = bf16[5120,128]{0,1:T(8,128)(2,1)} fusion(bf16[128,1536]{0,1:T(8,128)(2,1)S(1)} %bitcast.45, bf16[1536,5120]{1,0:T(8,128)(2,1)} %param.19), kind=kOutput, calls=%fused_computation.9 | convolution fusion | flops 2013921280 | bytes 17432576 | tf_op jit(solution)/shard_map/dot_general | solution.py:87
  265.4 0.0 reduce-scatter.2.cloned.1.call-update
  265.4 17.7 %all-gather.11.cloned.1.call-done = f32[32,3,5120]{2,1,0:T(4,128)} async-done(((f32[1,3,5120]{2,1,0:T(4,128)}), f32[32,3,5120]{2,1,0:T(4,128)}) %all-gather.11.cloned.1.call-update) | async-done | bytes 1966096 | tf_op jit(solution)/shard_map/all_gather | solution.py:45
  283.1 2.1 reduce_sum.54
  285.3 0.1 fusion.25
  285.4 7.3 %reduce-scatter.2.cloned.1.call-done = bf16[2560,128]{0,1:T(8,128)(2,1)} async-done(((bf16[5120,128]{0,1:T(8,128)(2,1)}), bf16[2560,128]{0,1:T(8,128)(2,1)}) %reduce-scatter.2.cloned.1.call-update) | async-done | bytes 655376 | tf_op jit(solution)/shard_map/reduce_scatter | solution.py:86
  292.7 0.0 copy-done.3
  292.7 1.3 fusion.12
  294.0 0.0 copy-start.1
  294.0 0.3 convert_reduce_fusion
  294.2 2.5 all-reduce
  296.7 1.3 fusion.10
  (7 shorter events, 0.0 us)
Async XLA Ops:
  7.2 8.7 %copy-start.2 = (bf16[128,1536]{1,0:T(8,128)(2,1)S(1)}, bf16[128,1536]{1,0:T(8,128)(2,1)}, u32[]{:S(2)}) copy-start(bf16[128,1536]{1,0:T(8,128)(2,1)} %param.12) | copy-start | bytes 1179652
  7.2 8.9 %copy-start.4 = (bf16[128,1536]{1,0:T(8,128)(2,1)S(1)}, bf16[128,1536]{1,0:T(8,128)(2,1)}, u32[]{:S(2)}) copy-start(bf16[128,1536]{1,0:T(8,128)(2,1)} %param.11) | copy-start | bytes 1179652
  7.2 54.8 %copy-start.6 = (f32[1536]{0:T(1024)S(1)}, f32[1536]{0:T(1024)}, u32[]{:S(2)}) copy-start(f32[1536]{0:T(1024)} %param.14) | copy-start | bytes 18436
  7.2 121.9 %copy-start.7 = (f32[1536]{0:T(1024)S(1)}, f32[1536]{0:T(1024)}, u32[]{:S(2)}) copy-start(f32[1536]{0:T(1024)} %param.15) | copy-start | bytes 18436
  7.2 121.9 %all-gather.7.cloned.1.call-start = ((), (), s32[]{:S(2)}) async-start(), calls=%async_computation.1 | async-start | bytes 6684672 | tf_op jit(solution)/shard_map/all_gather | solution.py:73
  9.2 214.2 %all-gather.9.cloned.1.call-start = ((), (), s32[]{:S(2)}) async-start(), calls=%async_computation.2 | async-start | bytes 6684672 | tf_op jit(solution)/shard_map/all_gather | solution.py:78
  10.0 273.1 %all-gather.11.cloned.1.call-start = ((), (), s32[]{:S(2)}) async-start(), calls=%async_computation.4 | async-start | bytes 2703360 | tf_op jit(solution)/shard_map/all_gather | solution.py:45
  15.8 276.9 %reduce-scatter.2.cloned.1.call-start = ((), (), s32[]{:S(2)}) async-start(), calls=%async_computation.3 | async-start | bytes 1966080 | tf_op jit(solution)/shard_map/reduce_scatter | solution.py:86
  237.0 4.6 %copy-start = (f32[12,2048,128]{2,1,0:T(8,128)}, f32[12,2048,128]{2,1,0:T(8,128)S(1)}, u32[]{:S(2)}) copy-start(f32[12,2048,128]{2,1,0:T(8,128)S(1)} %get-tuple-element.14) | copy-start | bytes 37748740
  256.2 29.0 %copy-start.5 = (f32[3,2560]{1,0:T(4,128)S(1)}, f32[3,2560]{1,0:T(4,128)}, u32[]{:S(2)}) copy-start(f32[3,2560]{1,0:T(4,128)} %param.18) | copy-start | bytes 92164
  256.2 36.5 %copy-start.3 = (bf16[128,2560]{1,0:T(8,128)(2,1)S(1)}, bf16[128,2560]{1,0:T(8,128)(2,1)}, u32[]{:S(2)}) copy-start(bf16[128,2560]{1,0:T(8,128)(2,1)} %param.10) | copy-start | bytes 1966084
  294.0 4.1 %copy-start.1 = (bf16[128,2560]{1,0:T(8,128)(2,1)}, bf16[128,2560]{1,0:T(8,128)(2,1)S(1)}, u32[]{:S(2)}) copy-start(bf16[128,2560]{1,0:T(8,128)(2,1)S(1)} %fusion.12) | copy-start | bytes 1966084
Sparse Core Ops, SparseCore 0:
  11.3 117.7 all-gather.6
  131.9 91.5 all-gather.8
  226.9 56.1 all-gather.10
  285.2 7.4 reduce-scatter.1
